TPU v7x, 512 devices: a whole 4x8x8 slice. The times are simulated.
512 devices in a mesh: ctx: 32 (over x, z_hi, core), tp: 16 (over y, z_lo).
Axes of the slice: x: 4, y: 8, z: 8 (z_hi: 4, z_lo: 2; z = z_hi * 2 + z_lo), core: 2. Of those that a mesh axis runs over, the one named last changes fastest.
Arguments:
- queries: bfloat16 [8192, 2048], P('ctx', 'tp'), may hold values from -24 to 24
- key_heads: bfloat16 [8192, 4, 128], P('ctx'), may hold values from -6 to 6
- head_values: bfloat16 [8192, 4, 128], P('ctx'), may hold values from -6 to 6
- hidden: bfloat16 [8192, 4096], P('ctx'), may hold values from -0.59765625 to 0.59765625
- out_proj: bfloat16 [2048, 4096], P('tp'), may hold values from -0.125 to 0.125
- norm_gain: float32 [4096], replicated, may hold values from 0.25 to 1.75
- x_proj: bfloat16 [4096, 4096], P('ctx', 'tp'), may hold values from -0.046875 to 0.046875
- bc_proj: bfloat16 [4096, 4, 256], P('ctx'), may hold values from -0.09375 to 0.09375
- dt_proj: bfloat16 [4096, 64], P('ctx', 'tp'), may hold values from -0.09375 to 0.09375
- dt_bias: float32 [64], P('tp'), may hold values from -12 to 0
- decay_log: float32 [64], P('tp'), may hold values from -10 to 3
- skip_gain: float32 [64], P('tp'), may hold values from 0.5 to 1.5
Outputs:
- residual_out: bfloat16 [8192, 4096], P('ctx', 'tp')
- mamba_out: bfloat16 [8192, 4096], P('ctx', 'tp')
All inputs are finite; a program needn't handle non-finite values.
Results may differ from a plain program's by a relative error of at most 0.034.
Values may be sent and summed in bfloat16 or wider, within the bound.
No kernel may reach another device: no remote copies, remote signals or barrier semaphores. Data moves between devices by JAX's collectives and lax.ppermute only.
A program may use at most 64 MiB of HBM per device.

v0:
```python
import math
import jax
import jax.numpy as jnp
from jax import lax
from jax.sharding import PartitionSpec as P


def prefix(value, axis, join, neutral, backward):
    count, mine = (lax.axis_size(axis), lax.axis_index(axis))
    pieces = jax.tree.map(lambda part: lax.all_gather(part, axis), value)
    if backward:
        pieces = jax.tree.map(lambda part: part[::-1], pieces)
        mine = count - 1 - mine
    so_far = jax.tree.map(
        lambda part, zero: jnp.full_like(part, 0) + jnp.asarray(zero, part.dtype), value, neutral
    )

    def lap(position, so_far):
        longer = join(so_far, jax.tree.map(lambda part: part[position], pieces))
        return jax.tree.map(lambda new, old: jnp.where(position < mine, new, old), longer, so_far)

    return lax.fori_loop(0, count - 1, lap, so_far)


def chain(earlier, later):
    return (earlier[0] * later[0], later[0][..., None, None] * earlier[1] + later[1])


def block_positions(rows, tok_dev, n_ctx):
    half = tok_dev // 2
    device = rows // tok_dev
    within = rows % tok_dev
    block = jnp.where(within < half, device, 2 * n_ctx - 1 - device)
    return block * half + within % half


def split_product(form, wide, narrow):
    upper = wide.astype(jnp.bfloat16)
    lower = (wide - upper.astype(jnp.float32)).astype(jnp.bfloat16)
    first_term = jnp.einsum(form, upper, narrow, preferred_element_type=jnp.float32)
    return first_term + jnp.einsum(form, lower, narrow, preferred_element_type=jnp.float32)


def body(
    queries,
    key_heads,
    head_values,
    hidden,
    out_proj,
    norm_gain,
    x_proj,
    bc_proj,
    dt_proj,
    dt_bias,
    decay_log,
    skip_gain,
):
    tok_dev = queries.shape[0]
    half = tok_dev // 2
    n_ctx = lax.axis_size("ctx")
    n_tp = lax.axis_size("tp")
    ctx_index = lax.axis_index("ctx")
    tp_index = lax.axis_index("tp")
    head_dim = key_heads.shape[2]
    kv_total = key_heads.shape[1]
    q_local = queries.shape[1] // head_dim
    group = q_local * n_tp // kv_total
    kv_local = max(1, q_local // group)
    per_kv = q_local // kv_local
    kv_start = tp_index * q_local // group
    keys_mine = lax.dynamic_slice_in_dim(key_heads, kv_start, kv_local, 1)
    values_mine = lax.dynamic_slice_in_dim(head_values, kv_start, kv_local, 1)
    query_pos = block_positions(
        ctx_index * tok_dev + jnp.arange(tok_dev, dtype=jnp.int32), tok_dev, n_ctx
    )
    shaped_q = queries.reshape(tok_dev, kv_local, per_kv, head_dim)
    root_dim = math.sqrt(head_dim)
    start_max = jnp.full((kv_local, per_kv, tok_dev), -1e30, jnp.float32)
    run_max = start_max
    key_piece = lax.all_gather(keys_mine, "ctx", axis=0, tiled=True)
    value_piece = lax.all_gather(values_mine, "ctx", axis=0, tiled=True)
    count = key_piece.shape[0]
    key_pos = block_positions(jnp.arange(count, dtype=jnp.int32), tok_dev, n_ctx)
    scores = (
        jnp.einsum("qgjd,kgd->gjqk", shaped_q, key_piece, preferred_element_type=jnp.float32)
        / root_dim
    )
    allowed = key_pos[None, :] <= query_pos[:, None]
    piece_max = jnp.max(jnp.where(allowed, scores, -1e30), axis=-1)
    new_max = jnp.maximum(run_max, piece_max)
    weights = jnp.where(allowed, jnp.exp(scores - new_max[..., None]), 0.0)
    run_sum = jnp.sum(weights, axis=-1)
    update = jnp.einsum(
        "gjqk,kgd->gjqd",
        weights.astype(jnp.bfloat16),
        value_piece,
        preferred_element_type=jnp.float32,
    )
    accum = update
    run_max, run_sum, accum = (new_max, run_sum, accum)
    attended = (
        jnp.transpose(accum / run_sum[..., None], (2, 0, 1, 3))
        .reshape(tok_dev, q_local * head_dim)
        .astype(jnp.bfloat16)
    )
    head_part = jnp.dot(attended, out_proj, preferred_element_type=jnp.float32)
    slice_width = hidden.shape[1] // n_tp
    attention_sum = lax.psum(head_part.astype(jnp.bfloat16), "tp").astype(jnp.float32)
    residual = (hidden.astype(jnp.float32) + attention_sum).astype(jnp.bfloat16)
    residual_out = lax.dynamic_slice_in_dim(residual, tp_index * slice_width, slice_width, 1)
    as_float = residual.astype(jnp.float32)
    mean_square = jnp.mean(as_float * as_float, axis=-1, keepdims=True)
    normed = (as_float * lax.rsqrt(mean_square + 1e-05) * norm_gain).astype(jnp.bfloat16)
    m_local = skip_gain.shape[0]
    state_size = bc_proj.shape[2] // 2
    groups_all = bc_proj.shape[1]
    per_group = m_local * n_tp // groups_all
    g_local = max(1, m_local // per_group)
    heads_each = m_local // g_local
    g_start = tp_index * m_local // per_group
    head_width = x_proj.shape[1] // m_local
    bc_mine = lax.dynamic_slice_in_dim(bc_proj, g_start, g_local, 1).reshape(
        bc_proj.shape[0], g_local * 2 * state_size
    )
    sum_x = jnp.dot(
        normed,
        lax.all_gather(x_proj, "ctx", axis=0, tiled=True),
        preferred_element_type=jnp.float32,
    )
    sum_bc = jnp.dot(
        normed,
        lax.all_gather(bc_mine, "ctx", axis=0, tiled=True),
        preferred_element_type=jnp.float32,
    )
    sum_dt = jnp.dot(
        normed,
        lax.all_gather(dt_proj, "ctx", axis=0, tiled=True),
        preferred_element_type=jnp.float32,
    )
    inputs_low = sum_x.astype(jnp.bfloat16).reshape(2, half, g_local, heads_each, head_width)
    inputs = inputs_low.astype(jnp.float32)
    bc_round = sum_bc.astype(jnp.bfloat16).reshape(2, half, g_local, 2 * state_size)
    b_low = bc_round[..., :state_size]
    c_low = bc_round[..., state_size:]
    steps = jax.nn.softplus(sum_dt + dt_bias).reshape(2, half, g_local, heads_each)
    rates = -jnp.exp(decay_log).reshape(g_local, heads_each)
    cumul = jnp.transpose(jnp.cumsum(steps * rates, axis=1), (0, 2, 3, 1))
    step_rows = jnp.transpose(steps, (0, 2, 3, 1))
    gram = jnp.einsum("ckgn,csgn->cgks", c_low, b_low, preferred_element_type=jnp.float32)
    places = jnp.arange(half, dtype=jnp.int32)
    causal = places[None, :] <= places[:, None]
    gaps = cumul[..., :, None] - cumul[..., None, :]
    decay = jnp.where(causal, jnp.exp(jnp.where(causal, gaps, 0.0)), 0.0)
    mixing = gram[:, :, None] * decay * step_rows[..., None, :]
    inner = split_product("cgjks,csgjp->ckgjp", mixing, inputs_low)
    last = cumul[..., -1]
    tail = jnp.exp(last[..., None] - cumul) * step_rows
    weighted = jnp.transpose(tail, (0, 3, 1, 2))[..., None] * inputs
    block_state = split_product("csgjp,csgn->cgjpn", weighted, b_low)
    block_decay = jnp.exp(last)
    first = (block_decay[0], block_state[0])
    second = (block_decay[1], block_state[1])
    unit = (jnp.ones_like(first[0]), jnp.zeros_like(first[1]))
    before = prefix(first, "ctx", chain, unit, False)
    last_device = ctx_index == n_ctx - 1
    through = chain(before, first)
    joined = chain(through, second)
    sent = (
        jnp.where(last_device, joined[0], second[0]),
        jnp.where(last_device, joined[1], second[1]),
    )
    after = prefix(sent, "ctx", chain, unit, True)
    second_in = jnp.where(last_device, through[1], after[1])
    entering = jnp.stack([before[1], second_in])
    carried = jnp.transpose(jnp.exp(cumul), (0, 3, 1, 2))[..., None] * split_product(
        "cgjpn,ckgn->ckgjp", entering, c_low
    )
    output = inner + carried + skip_gain.reshape(g_local, heads_each)[:, :, None] * inputs
    mamba_out = output.reshape(tok_dev, m_local * head_width).astype(jnp.bfloat16)
    return (residual_out, mamba_out)


def solution(mesh):
    placed = (
        P("ctx", "tp"),
        P("ctx", None, None),
        P("ctx", None, None),
        P("ctx", None),
        P("tp", None),
        P(),
        P("ctx", "tp"),
        P("ctx", None, None),
        P("ctx", "tp"),
        P("tp"),
        P("tp"),
        P("tp"),
    )
    return jax.shard_map(
        body,
        mesh=mesh,
        in_specs=placed,
        out_specs=(P("ctx", "tp"), P("ctx", "tp")),
        check_vma=False,
    )
```

profile of v0, /device:TPU:1, one launch (start us, length us, event | category | flops | bytes accessed | tf_op | source)
XLA Modules:
  0.0 671.6 jit_solution(12906673132283992635)
XLA Ops:
  11.0 66.9 %all-gather.13.cloned.1.call-done = bf16[8192,1,128]{2,0,1:T(8,128)(2,1)} async-done(((bf16[256,1,128]{2,0,1:T(8,128)(2,1)}), bf16[8192,1,128]{2,0,1:T(8,128)(2,1)}) %all-gather.13.cloned.1.call-update) | async-done | bytes 2097168 | tf_op jit(solution)/shard_map/all_gather | solution.py:80
  77.9 5.7 fusion.4
  83.6 3.3 copy-done.1
  86.9 3.7 fusion.5
  90.7 48.6 %all-gather.15.cloned.1.call-done = bf16[8192,1,128]{2,0,1:T(8,128)(2,1)} async-done(((bf16[256,1,128]{2,0,1:T(8,128)(2,1)}), bf16[8192,1,128]{2,0,1:T(8,128)(2,1)}) %all-gather.15.cloned.1.call-update) | async-done | bytes 2097168 | tf_op jit(solution)/shard_map/all_gather | solution.py:81
  139.3 8.7 %convolution_convert_fusion = bf16[256,4096]{1,0:T(8,128)(2,1)} fusion(bf16[128,4096]{1,0:T(8,128)(2,1)S(1)} %copy-done, bf16[8192,1,128]{2,0,1:T(8,128)(2,1)} %all-gather.15.cloned.1.call-done, f32[1,1,256,8192]{2,3,1,0:T(8,128)} %copy-done.1, f32[256]{0:T(256)S(1)} %broadcast_maximum_fusion, s32[256]{0:T(256)S(1)} %fusion.88, s32[8192]{0:T(1024)S(1)} %fusion.83, ...), kind=kOutput, calls=%fused_computation.18 | convolution fusion | flops 814809088 | bytes 13667328 | tf_op jit(solution)/shard_map/dot_general | solution.py:106
  149.5 43.0 %all_gather.37 = bf16[4096,4]{0,1:T(4,128)(2,1)S(1)} all-gather(bf16[128,4]{0,1:T(4,128)(2,1)S(1)} %copy-done.14), channel_id=1, replica_groups=mesh['ctx'=32,'tp'=16] {'ctx'}, dimensions={0}, use_global_device_ids=true | all-gather | bytes 33792 | tf_op jit(solution)/shard_map/all_gather | solution.py:137
  192.5 94.5 %all-reduce.2.cloned.1.call-done = bf16[256,4096]{1,0:T(8,128)(2,1)} async-done(((bf16[256,4096]{1,0:T(8,128)(2,1)}), bf16[256,4096]{1,0:T(8,128)(2,1)}) %all-reduce.2.cloned.1.call-update) | async-done | bytes 2097168 | tf_op jit(solution)/shard_map/psum | solution.py:108
  287.0 3.2 fusion.7
  290.2 68.7 %all-gather.17.cloned.1.call-done = bf16[4096,256]{1,0:T(8,128)(2,1)} async-done(((bf16[128,256]{1,0:T(8,128)(2,1)}), bf16[4096,256]{1,0:T(8,128)(2,1)}) %all-gather.17.cloned.1.call-update) | async-done | bytes 2097168 | tf_op jit(solution)/shard_map/all_gather | solution.py:127
  358.9 2.4 convolution_convert_fusion.1
  365.1 55.0 %all-gather.19.cloned.1.call-done = bf16[4096,1,256]{2,0,1:T(8,128)(2,1)} async-done(((bf16[128,1,256]{2,0,1:T(8,128)(2,1)}), bf16[4096,1,256]{2,0,1:T(8,128)(2,1)}) %all-gather.19.cloned.1.call-update) | async-done | bytes 2097168 | tf_op jit(solution)/shard_map/all_gather | solution.py:132
  420.1 2.4 fusion.24
  425.6 43.8 %all-gather.1 = f32[32,1,4,1]{2,3,1,0:T(1,128)} all-gather(f32[1,1,4,1]{2,3,1,0:T(1,128)S(1)} %get-tuple-element.328), channel_id=3, replica_groups=mesh['ctx'=32,'tp'=16] {'ctx'}, dimensions={0}, use_global_device_ids=true | all-gather | bytes 528 | tf_op jit(solution)/shard_map/all_gather | solution.py:10
  469.4 19.7 %all-gather.21.cloned.1.call-done = f32[32,4,64,128]{3,2,1,0:T(8,128)} async-done(((f32[1,4,64,128]{3,2,1,0:T(8,128)}), f32[32,4,64,128]{3,2,1,0:T(8,128)}) %all-gather.21.cloned.1.call-update) | async-done | bytes 4194320 | tf_op jit(solution)/shard_map/all_gather | solution.py:10
  489.1 70.9 %while.30 = (s32[]{:T(128)}, f32[1,4]{1,0:T(1,128)S(1)}, f32[1,4,64,128]{3,2,1,0:T(8,128)S(1)}, s32[]{:T(128)}, f32[32,1,4]{2,1,0:T(1,128)}, /*index=5*/f32[32,1,4,64,128]{4,3,2,1,0:T(8,128)}, s32[]{:T(128)}, s32[]{:T(128)}) while((s32[]{:T(128)}, f32[1,4]{1,0:T(1,128)S(1)}, f32[1,4,64,128]{3,2,1,0:T(8,128)S(1)}, s32[]{:T(128)}, ...), condition=%wide.region_6.7_spmd.clone, body=%wide.region_5.6_spmd.clone.sunk | while | flops 131088 | bytes 393431 | solution.py:22
  560.0 1.3 add_select_fusion
  561.4 2.0 reshape.405
  564.3 2.0 copy.102
  568.0 1.3 fusion.50
  570.0 42.2 %all-gather.5 = f32[32,1,4]{2,1,0:T(1,128)S(1)} all-gather(f32[1,1,4]{2,1,0:T(1,128)S(1)} %fusion.91), channel_id=5, replica_groups=mesh['ctx'=32,'tp'=16] {'ctx'}, dimensions={0}, use_global_device_ids=true | all-gather | bytes 528 | tf_op jit(solution)/shard_map/all_gather | solution.py:10
  612.5 13.4 %all-gather.23.cloned.1.call-done = f32[32,4,64,128]{3,2,1,0:T(8,128)} async-done(((f32[1,4,64,128]{3,2,1,0:T(8,128)}), f32[32,4,64,128]{3,2,1,0:T(8,128)}) %all-gather.23.cloned.1.call-update) | async-done | bytes 4194320 | tf_op jit(solution)/shard_map/all_gather | solution.py:10
  625.9 4.8 reverse_bitcast_fusion
  630.7 32.0 %while.31 = (s32[]{:T(128)}, f32[1,4,64,128]{3,2,1,0:T(8,128)S(1)}, s32[]{:T(128)}, f32[32,1,4]{2,1,0:T(1,128)S(1)}, f32[32,1,4,64,128]{4,3,2,1,0:T(8,128)}, /*index=5*/s32[]{:T(128)}, s32[]{:T(128)}) while((s32[]{:T(128)}, f32[1,4,64,128]{3,2,1,0:T(8,128)S(1)}, s32[]{:T(128)}, f32[32,1,4]{2,1,0:T(1,128)S(1)}, ...), condition=%wide.region_8.9_spmd.clone, body=%wide.region_7.8_spmd.clone.sunk | while | flops 131076 | bytes 393369 | solution.py:22
  (250 shorter events, 119.3 us)
Async XLA Ops:
  7.2 132.1 %copy-start = (bf16[128,4096]{1,0:T(8,128)(2,1)S(1)}, bf16[128,4096]{1,0:T(8,128)(2,1)}, u32[]{:S(2)}) copy-start(bf16[128,4096]{1,0:T(8,128)(2,1)} %param.20) | copy-start | bytes 3145732
  7.2 70.7 %all-gather.13.cloned.1.call-start = ((), (), s32[]{:S(2)}) async-start(), calls=%async_computation | async-start | bytes 2162688 | tf_op jit(solution)/shard_map/all_gather | solution.py:80
  9.1 130.2 %all-gather.15.cloned.1.call-start = ((), (), s32[]{:S(2)}) async-start(), calls=%async_computation.1 | async-start | bytes 2162688 | tf_op jit(solution)/shard_map/all_gather | solution.py:81
  10.9 276.1 %all-reduce.2.cloned.1.call-start = ((), (), s32[]{:S(2)}) async-start(), calls=%async_computation.2 | async-start | bytes 4194304 | tf_op jit(solution)/shard_map/psum | solution.py:108
  90.6 58.0 %copy-start.11 = (bf16[128,4,256]{2,1,0:T(4,128)(2,1)S(1)}, bf16[128,4,256]{2,1,0:T(4,128)(2,1)}, u32[]{:S(2)}) copy-start(bf16[128,4,256]{2,1,0:T(4,128)(2,1)} %param.23) | copy-start | bytes 786436
  90.6 58.9 %copy-start.14 = (bf16[128,4]{0,1:T(4,128)(2,1)S(1)}, bf16[128,4]{0,1:T(4,128)(2,1)}, u32[]{:S(2)}) copy-start(bf16[128,4]{0,1:T(4,128)(2,1)} %param.24) | copy-start | bytes 3076
  90.6 101.8 %copy-start.17 = (f32[4]{0:T(128)S(1)}, f32[4]{0:T(128)}, u32[]{:S(2)}) copy-start(f32[4]{0:T(128)} %param.26) | copy-start | bytes 52
  148.0 210.9 %copy-start.16 = (f32[4096]{0:T(1024)S(1)}, f32[4096]{0:T(1024)}, u32[]{:S(2)}) copy-start(f32[4096]{0:T(1024)} %param.21) | copy-start | bytes 49156
  148.0 210.9 %all-gather.17.cloned.1.call-start = ((), (), s32[]{:S(2)}) async-start(), calls=%async_computation.3 | async-start | bytes 2162688 | tf_op jit(solution)/shard_map/all_gather | solution.py:127
  148.6 271.5 %all-gather.19.cloned.1.call-start = ((), (), s32[]{:S(2)}) async-start(), calls=%async_computation.4 | async-start | bytes 2162688 | tf_op jit(solution)/shard_map/all_gather | solution.py:132
  149.4 339.7 %all-gather.21.cloned.1.call-start = ((), (), s32[]{:S(2)}) async-start(), calls=%async_computation.5 | async-start | bytes 4325376 | tf_op jit(solution)/shard_map/all_gather | solution.py:10
  290.2 73.0 %copy-start.18 = (f32[4]{0:T(128)S(1)}, f32[4]{0:T(128)}, u32[]{:S(2)}) copy-start(f32[4]{0:T(128)} %param.25) | copy-start | bytes 52
  290.2 73.8 %copy-start.15 = (f32[256]{0:T(256)}, f32[256]{0:T(256)S(1)}, u32[]{:S(2)}) copy-start(f32[256]{0:T(256)S(1)} %add_rsqrt_fusion) | copy-start | bytes 3076
  363.2 59.3 %copy-start.5 = (bf16[2,128,4,64]{1,3,2,0:T(8,128)(2,1)}, bf16[2,128,4,64]{1,3,2,0:T(8,128)(2,1)S(1)}, u32[]{:S(2)}) copy-start(bf16[2,128,4,64]{1,3,2,0:T(8,128)(2,1)S(1)} %copy.90) | copy-start | bytes 393220
  364.3 60.6 %copy-start.4 = (f32[2,128,1,4]{3,2,1,0:T(1,128)}, f32[2,128,1,4]{3,2,1,0:T(1,128)S(1)}, u32[]{:S(2)}) copy-start(f32[2,128,1,4]{3,2,1,0:T(1,128)S(1)} %fusion.59) | copy-start | bytes 12292
  365.1 60.0 %copy-start.12 = (f32[2,1,4,1]{2,1,3,0:T(1,128)S(1)}, f32[2,1,4,1]{2,1,3,0:T(1,128)}, u32[]{:S(2)}) copy-start(f32[2,1,4,1]{2,1,3,0:T(1,128)} %get-tuple-element.323) | copy-start | bytes 100
  424.2 137.1 %copy-start.2 = (f32[2,4,64,128]{3,2,1,0:T(8,128)}, f32[2,4,64,128]{3,2,1,0:T(8,128)S(1)}, u32[]{:S(2)}) copy-start(f32[2,4,64,128]{3,2,1,0:T(8,128)S(1)} %convolution_add_fusion.1) | copy-start | bytes 786436
  425.0 201.0 %all-gather.23.cloned.1.call-start = ((), (), s32[]{:S(2)}) async-start(), calls=%async_computation.6 | async-start | bytes 4325376 | tf_op jit(solution)/shard_map/all_gather | solution.py:10
  612.5 50.3 %copy-start.3 = (f32[2,4,64,128]{3,2,1,0:T(8,128)S(1)}, f32[2,4,64,128]{3,2,1,0:T(8,128)}, u32[]{:S(2)}) copy-start(f32[2,4,64,128]{3,2,1,0:T(8,128)} %copy-done.2) | copy-start | bytes 786436
  612.5 50.3 %copy-start.13 = (f32[4]{0:T(128)S(1)}, f32[4]{0:T(128)}, u32[]{:S(2)}) copy-start(f32[4]{0:T(128)} %get-tuple-element.326) | copy-start | bytes 52
  612.5 50.4 %copy-start.8 = (bf16[256,256]{1,0:T(8,128)(2,1)S(1)}, bf16[256,256]{1,0:T(8,128)(2,1)}, u32[]{:S(2)}) copy-start(bf16[256,256]{1,0:T(8,128)(2,1)} %copy-done.7) | copy-start | bytes 393220
  612.5 50.8 %copy-start.6 = (bf16[2,128,4,64]{1,3,2,0:T(8,128)(2,1)S(1)}, bf16[2,128,4,64]{1,3,2,0:T(8,128)(2,1)}, u32[]{:S(2)}) copy-start(bf16[2,128,4,64]{1,3,2,0:T(8,128)(2,1)} %copy-done.5) | copy-start | bytes 393220
  612.5 50.8 %copy-start.10 = (f32[2,128,1,4,64]{1,4,3,0,2:T(8,128)S(1)}, f32[2,128,1,4,64]{1,4,3,0,2:T(8,128)}, u32[]{:S(2)}) copy-start(f32[2,128,1,4,64]{1,4,3,0,2:T(8,128)} %copy.102) | copy-start | bytes 786436
  612.5 50.8 %copy-start.19 = (f32[4]{0:T(128)S(1)}, f32[4]{0:T(128)}, u32[]{:S(2)}) copy-start(f32[4]{0:T(128)} %param.27) | copy-start | bytes 52
  (3 other events, 6.7 us)
Sparse Core Ops, SparseCore 0:
  11.7 66.1 all-gather.12
  81.6 57.6 all-gather.14
  148.1 138.8 all-reduce.1
  290.0 68.8 all-gather.16
  362.4 57.6 all-gather.18
  425.1 63.9 all-gather.20
  561.5 64.4 all-gather.22
where the time goes:
time: 674 us; the launch traced here: 672 us
  waiting for transfers between devices  368 us (55%)
  blocking collectives  129 us (19%)
  other arithmetic  91 us (14%)
  local copies, waits for them, and re-layouts  43.9 us (7%)
  matrix products  24.1 us (4%)
  between operations  14.6 us (2%)
    psum x1, waiting for transfers between devices, body(): lax.psum(head_part.astype(jnp.bfloat16), 'tp').astype(jnp.float32)  94.5 us
    all_gather x2, blocking collectives, prefix(): pieces = jax.tree.map(lambda part: lax.all_gather(part, axis), value)  86.1 us
    select_n x93, other arithmetic, lap(): jnp.where(position < mine, new, old)  81.7 us
    all_gather x1, waiting for transfers between devices, body(): lax.all_gather(x_proj, 'ctx', axis=0, tiled=True)  68.7 us
    all_gather x1, waiting for transfers between devices, body(): key_piece = lax.all_gather(keys_mine, 'ctx', axis=0, tiled=True)  66.9 us
    all_gather x1, waiting for transfers between devices, body(): lax.all_gather(bc_mine, 'ctx', axis=0, tiled=True)  55 us
    all_gather x1, waiting for transfers between devices, body(): value_piece = lax.all_gather(values_mine, 'ctx', axis=0, tiled=True)  48.6 us
    all_gather x1, blocking collectives, body(): lax.all_gather(dt_proj, 'ctx', axis=0, tiled=True)  43 us
  transfers between devices with their start and end apart: 7, of which 7 were waited for; matrix products, arithmetic and copies ran while one was open for 5% of the time, Pallas kernels for 0%

commit v1 on v0

--- a/solution.py
+++ b/solution.py
@@ -105,7 +105,9 @@
     )
     head_part = jnp.dot(attended, out_proj, preferred_element_type=jnp.float32)
     slice_width = hidden.shape[1] // n_tp
-    attention_sum = lax.psum(head_part.astype(jnp.bfloat16), "tp").astype(jnp.float32)
+    attention_sum = jnp.sum(lax.all_gather(head_part.astype(jnp.bfloat16), "tp"), axis=0).astype(
+        jnp.float32
+    )
     residual = (hidden.astype(jnp.float32) + attention_sum).astype(jnp.bfloat16)
     residual_out = lax.dynamic_slice_in_dim(residual, tp_index * slice_width, slice_width, 1)
     as_float = residual.astype(jnp.float32)

time: 674 us -> 1170 us (1.74)
  waiting for transfers between devices: 368 us -> 880 us
  local copies, waits for them, and re-layouts: 43.9 us -> 18.9 us
  blocking collectives: 129 us -> 151 us
    all_gather x0 -> x1, waiting for transfers between devices: none -> 621 us  [body(): lax.all_gather(head_part.astype(jnp.bfloat16), 'tp')]
    psum x1 -> x0, waiting for transfers between devices: 94.5 us -> none  [body(): lax.psum(head_part.astype(jnp.bfloat16), 'tp').astype(jnp.float32)]
    all_gather x1, blocking collectives: 43 us -> 66.3 us  [body(): lax.all_gather(dt_proj, 'ctx', axis=0, tiled=True)]
    all_gather x1, waiting for transfers between devices: 68.7 us -> 48.4 us  [body(): lax.all_gather(x_proj, 'ctx', axis=0, tiled=True)]
    mul x63, local copies, waits for them, and re-layouts: 20.6 us -> 0.42 us  [chain(): later[0][..., None, None] * earlier[1] + later[1]]
    select_n x93, other arithmetic: 81.7 us -> 62.1 us  [lap(): jnp.where(position < mine, new, old)]
  transfers between devices with their start and end apart: 7 -> 7, of which waited for: 7 -> 7; matrix products, arithmetic and copies ran while one was open for 5% -> 3% of each run, Pallas kernels for 0% -> 0%
where the time goes in v1:
time: 1170 us
  waiting for transfers between devices  880 us (75%)
  blocking collectives  151 us (13%)
  other arithmetic  83.1 us (7%)
  matrix products  22.8 us (2%)
  local copies, waits for them, and re-layouts  18.9 us (2%)
  between operations  14.6 us (1%)
    all_gather x1, waiting for transfers between devices, body(): lax.all_gather(head_part.astype(jnp.bfloat16), 'tp')  621 us
    all_gather x2, blocking collectives, prefix(): pieces = jax.tree.map(lambda part: lax.all_gather(part, axis), value)  84.5 us
    all_gather x1, waiting for transfers between devices, body(): key_piece = lax.all_gather(keys_mine, 'ctx', axis=0, tiled=True)  66.9 us
    all_gather x1, blocking collectives, body(): lax.all_gather(dt_proj, 'ctx', axis=0, tiled=True)  66.3 us
    select_n x93, other arithmetic, lap(): jnp.where(position < mine, new, old)  62.1 us
    all_gather x1, waiting for transfers between devices, body(): lax.all_gather(bc_mine, 'ctx', axis=0, tiled=True)  56.7 us
    all_gather x1, waiting for transfers between devices, body(): value_piece = lax.all_gather(values_mine, 'ctx', axis=0, tiled=True)  48.7 us
    all_gather x1, waiting for transfers between devices, body(): lax.all_gather(x_proj, 'ctx', axis=0, tiled=True)  48.4 us
  transfers between devices with their start and end apart: 7, of which 7 were waited for; matrix products, arithmetic and copies ran while one was open for 3% of the time, Pallas kernels for 0%

profile of v1, /device:TPU:1, one launch (start us, length us, event | category | flops | bytes accessed | tf_op | source)
XLA Modules:
  0.0 1172.8 jit_solution(13169927894742688786)
XLA Ops:
  7.2 1.2 constant_dynamic-slice_fusion.4
  11.0 66.9 %all-gather.15.cloned.1.call-done = bf16[8192,1,128]{2,0,1:T(8,128)(2,1)} async-done(((bf16[256,1,128]{2,0,1:T(8,128)(2,1)}), bf16[8192,1,128]{2,0,1:T(8,128)(2,1)}) %all-gather.15.cloned.1.call-update) | async-done | bytes 2097168 | tf_op jit(solution)/shard_map/all_gather | solution.py:80
  77.9 5.7 fusion.4
  83.6 3.2 copy-done.2
  86.9 3.7 fusion.5
  90.6 48.7 %all-gather.17.cloned.1.call-done = bf16[8192,1,128]{2,0,1:T(8,128)(2,1)} async-done(((bf16[256,1,128]{2,0,1:T(8,128)(2,1)}), bf16[8192,1,128]{2,0,1:T(8,128)(2,1)}) %all-gather.17.cloned.1.call-update) | async-done | bytes 2097168 | tf_op jit(solution)/shard_map/all_gather | solution.py:81
  139.3 8.6 convolution_convert_fusion
  149.5 66.3 %all_gather.45 = bf16[4096,4]{0,1:T(4,128)(2,1)S(1)} all-gather(bf16[128,4]{0,1:T(4,128)(2,1)S(1)} %copy-done.17), channel_id=1, replica_groups=mesh['ctx'=32,'tp'=16] {'ctx'}, dimensions={0}, use_global_device_ids=true | all-gather | bytes 33792 | tf_op jit(solution)/shard_map/all_gather | solution.py:139
  215.8 620.6 %all-gather.21.cloned.1.call-done = bf16[4096,4096]{1,0:T(8,128)(2,1)} async-done(((bf16[256,4096]{1,0:T(8,128)(2,1)}), bf16[4096,4096]{1,0:T(8,128)(2,1)}) %all-gather.21.cloned.1.call-update) | async-done | bytes 33554448 | tf_op jit(solution)/shard_map/all_gather | solution.py:108
  836.3 11.7 reduce_sum.31
  848.0 3.9 fusion.7
  851.9 48.4 %all-gather.19.cloned.1.call-done = bf16[4096,256]{1,0:T(8,128)(2,1)} async-done(((bf16[128,256]{1,0:T(8,128)(2,1)}), bf16[4096,256]{1,0:T(8,128)(2,1)}) %all-gather.19.cloned.1.call-update) | async-done | bytes 2097168 | tf_op jit(solution)/shard_map/all_gather | solution.py:129
  900.4 3.0 convolution_convert_fusion.1
  904.9 56.7 %all-gather.23.cloned.1.call-done = bf16[4096,1,256]{2,0,1:T(8,128)(2,1)} async-done(((bf16[128,1,256]{2,0,1:T(8,128)(2,1)}), bf16[4096,1,256]{2,0,1:T(8,128)(2,1)}) %all-gather.23.cloned.1.call-update) | async-done | bytes 2097168 | tf_op jit(solution)/shard_map/all_gather | solution.py:134
  961.6 2.4 fusion.24
  965.2 42.3 %all-gather.2 = f32[32,1,4,1]{2,3,1,0:T(1,128)S(1)} all-gather(f32[1,1,4,1]{2,3,1,0:T(1,128)S(1)} %get-tuple-element.328), channel_id=4, replica_groups=mesh['ctx'=32,'tp'=16] {'ctx'}, dimensions={0}, use_global_device_ids=true | all-gather | bytes 528 | tf_op jit(solution)/shard_map/all_gather | solution.py:10
  1007.4 21.7 %all-gather.25.cloned.1.call-done = f32[32,4,64,128]{3,2,1,0:T(8,128)} async-done(((f32[1,4,64,128]{3,2,1,0:T(8,128)}), f32[32,4,64,128]{3,2,1,0:T(8,128)}) %all-gather.25.cloned.1.call-update) | async-done | bytes 4194320 | tf_op jit(solution)/shard_map/all_gather | solution.py:10
  1029.1 32.6 %while.30 = (s32[]{:T(128)}, f32[1,4]{1,0:T(1,128)S(1)}, f32[1,4,64,128]{3,2,1,0:T(8,128)S(1)}, s32[]{:T(128)}, f32[32,1,4]{2,1,0:T(1,128)S(1)}, /*index=5*/f32[32,1,4,64,128]{4,3,2,1,0:T(8,128)}, s32[]{:T(128)}, s32[]{:T(128)}) while((s32[]{:T(128)}, f32[1,4]{1,0:T(1,128)S(1)}, f32[1,4,64,128]{3,2,1,0:T(8,128)S(1)}, s32[]{:T(128)}, ...), condition=%wide.region_6.7_spmd.clone, body=%wide.region_5.6_spmd.clone.sunk | while | flops 131088 | bytes 393431 | solution.py:22
  1063.1 1.2 reshape.406
  1066.7 1.1 fusion.50
  1067.9 42.2 %all-gather.6 = f32[32,1,4]{2,1,0:T(1,128)S(1)} all-gather(f32[1,1,4]{2,1,0:T(1,128)S(1)} %fusion.91), channel_id=6, replica_groups=mesh['ctx'=32,'tp'=16] {'ctx'}, dimensions={0}, use_global_device_ids=true | all-gather | bytes 528 | tf_op jit(solution)/shard_map/all_gather | solution.py:10
  1110.4 16.7 %all-gather.27.cloned.1.call-done = f32[32,4,64,128]{3,2,1,0:T(8,128)} async-done(((f32[1,4,64,128]{3,2,1,0:T(8,128)}), f32[32,4,64,128]{3,2,1,0:T(8,128)}) %all-gather.27.cloned.1.call-update) | async-done | bytes 4194320 | tf_op jit(solution)/shard_map/all_gather | solution.py:10
  1127.1 4.8 reverse_bitcast_fusion
  1132.0 32.0 %while.31 = (s32[]{:T(128)}, f32[1,4,64,128]{3,2,1,0:T(8,128)S(1)}, s32[]{:T(128)}, f32[32,1,4]{2,1,0:T(1,128)S(1)}, f32[32,1,4,64,128]{4,3,2,1,0:T(8,128)}, /*index=5*/s32[]{:T(128)}, s32[]{:T(128)}) while((s32[]{:T(128)}, f32[1,4,64,128]{3,2,1,0:T(8,128)S(1)}, s32[]{:T(128)}, f32[32,1,4]{2,1,0:T(1,128)S(1)}, ...), condition=%wide.region_8.9_spmd.clone, body=%wide.region_7.8_spmd.clone.sunk | while | flops 131076 | bytes 393369 | solution.py:22
  (255 shorter events, 75.2 us)
Async XLA Ops:
  7.2 132.1 %copy-start = (bf16[128,4096]{1,0:T(8,128)(2,1)S(1)}, bf16[128,4096]{1,0:T(8,128)(2,1)}, u32[]{:S(2)}) copy-start(bf16[128,4096]{1,0:T(8,128)(2,1)} %param.20) | copy-start | bytes 3145732
  7.2 70.7 %all-gather.15.cloned.1.call-start = ((), (), s32[]{:S(2)}) async-start(), calls=%async_computation | async-start | bytes 2162688 | tf_op jit(solution)/shard_map/all_gather | solution.py:80
  9.1 130.2 %all-gather.17.cloned.1.call-start = ((), (), s32[]{:S(2)}) async-start(), calls=%async_computation.1 | async-start | bytes 2162688 | tf_op jit(solution)/shard_map/all_gather | solution.py:81
  10.9 825.4 %all-gather.21.cloned.1.call-start = ((), (), s32[]{:S(2)}) async-start(), calls=%async_computation.3 | async-start | bytes 35651584 | tf_op jit(solution)/shard_map/all_gather | solution.py:108
  90.6 58.0 %copy-start.10 = (bf16[128,4,256]{2,1,0:T(4,128)(2,1)S(1)}, bf16[128,4,256]{2,1,0:T(4,128)(2,1)}, u32[]{:S(2)}) copy-start(bf16[128,4,256]{2,1,0:T(4,128)(2,1)} %param.23) | copy-start | bytes 786436
  90.6 58.9 %copy-start.17 = (bf16[128,4]{0,1:T(4,128)(2,1)S(1)}, bf16[128,4]{0,1:T(4,128)(2,1)}, u32[]{:S(2)}) copy-start(bf16[128,4]{0,1:T(4,128)(2,1)} %param.24) | copy-start | bytes 3076
  90.6 125.2 %copy-start.19 = (f32[4]{0:T(128)S(1)}, f32[4]{0:T(128)}, u32[]{:S(2)}) copy-start(f32[4]{0:T(128)} %param.26) | copy-start | bytes 52
  148.0 752.4 %all-gather.19.cloned.1.call-start = ((), (), s32[]{:S(2)}) async-start(), calls=%async_computation.2 | async-start | bytes 2162688 | tf_op jit(solution)/shard_map/all_gather | solution.py:129
  148.5 813.0 %all-gather.23.cloned.1.call-start = ((), (), s32[]{:S(2)}) async-start(), calls=%async_computation.4 | async-start | bytes 2162688 | tf_op jit(solution)/shard_map/all_gather | solution.py:134
  149.4 879.7 %all-gather.25.cloned.1.call-start = ((), (), s32[]{:S(2)}) async-start(), calls=%async_computation.5 | async-start | bytes 4325376 | tf_op jit(solution)/shard_map/all_gather | solution.py:10
  848.0 52.4 %copy-start.18 = (f32[4096]{0:T(1024)S(1)}, f32[4096]{0:T(1024)}, u32[]{:S(2)}) copy-start(f32[4096]{0:T(1024)} %param.21) | copy-start | bytes 49156
  851.9 51.8 %copy-start.20 = (f32[4]{0:T(128)S(1)}, f32[4]{0:T(128)}, u32[]{:S(2)}) copy-start(f32[4]{0:T(128)} %param.25) | copy-start | bytes 52
  903.4 60.6 %copy-start.8 = (bf16[256,256]{1,0:T(8,128)(2,1)}, bf16[256,256]{1,0:T(8,128)(2,1)S(1)}, u32[]{:S(2)}) copy-start(bf16[256,256]{1,0:T(8,128)(2,1)S(1)} %convolution_convert_fusion.1) | copy-start | bytes 393220
  964.0 146.3 %copy-start.6 = (bf16[256,256]{1,0:T(8,128)(2,1)}, bf16[256,256]{1,0:T(8,128)(2,1)S(1)}, u32[]{:S(2)}) copy-start(bf16[256,256]{1,0:T(8,128)(2,1)S(1)} %fusion.24) | copy-start | bytes 393220
  964.3 102.3 %copy-start.4 = (f32[2,4,64,128]{3,2,1,0:T(8,128)}, f32[2,4,64,128]{3,2,1,0:T(8,128)S(1)}, u32[]{:S(2)}) copy-start(f32[2,4,64,128]{3,2,1,0:T(8,128)S(1)} %convolution_add_fusion.1) | copy-start | bytes 786436
  965.1 162.1 %all-gather.27.cloned.1.call-start = ((), (), s32[]{:S(2)}) async-start(), calls=%async_computation.6 | async-start | bytes 4325376 | tf_op jit(solution)/shard_map/all_gather | solution.py:10
  965.1 97.4 %copy-start.12 = (f32[4]{0:T(128)}, f32[4]{0:T(128)S(1)}, u32[]{:S(2)}) copy-start(f32[4]{0:T(128)S(1)} %get-tuple-element.326) | copy-start | bytes 52
  1110.4 53.6 %copy-start.5 = (f32[2,4,64,128]{3,2,1,0:T(8,128)S(1)}, f32[2,4,64,128]{3,2,1,0:T(8,128)}, u32[]{:S(2)}) copy-start(f32[2,4,64,128]{3,2,1,0:T(8,128)} %copy-done.4) | copy-start | bytes 786436
  1110.4 53.6 %copy-start.13 = (f32[4]{0:T(128)S(1)}, f32[4]{0:T(128)}, u32[]{:S(2)}) copy-start(f32[4]{0:T(128)} %copy-done.12) | copy-start | bytes 52
  1110.4 53.7 %copy-start.7 = (bf16[256,256]{1,0:T(8,128)(2,1)S(1)}, bf16[256,256]{1,0:T(8,128)(2,1)}, u32[]{:S(2)}) copy-start(bf16[256,256]{1,0:T(8,128)(2,1)} %copy-done.6) | copy-start | bytes 393220
  1110.4 54.0 %copy-start.9 = (f32[2,128,1,4,64]{1,4,3,0,2:T(8,128)S(1)}, f32[2,128,1,4,64]{1,4,3,0,2:T(8,128)}, u32[]{:S(2)}) copy-start(f32[2,128,1,4,64]{1,4,3,0,2:T(8,128)} %copy.102) | copy-start | bytes 786436
  1110.4 54.0 %copy-start.11 = (pred[128,128]{1,0:T(8,128)(4,1)S(1)}, pred[128,128]{1,0:T(8,128)(4,1)}, u32[]{:S(2)}) copy-start(pred[128,128]{1,0:T(8,128)(4,1)} %iota_compare_fusion) | copy-start | bytes 49156
  1110.4 54.0 %copy-start.14 = (f32[2,4,128]{2,1,0:T(4,128)S(1)}, f32[2,4,128]{2,1,0:T(4,128)}, u32[]{:S(2)}) copy-start(f32[2,4,128]{2,1,0:T(4,128)} %copy.87) | copy-start | bytes 12292
  1110.4 54.0 %copy-start.21 = (f32[4]{0:T(128)S(1)}, f32[4]{0:T(128)}, u32[]{:S(2)}) copy-start(f32[4]{0:T(128)} %param.27) | copy-start | bytes 52
  (5 other events, 176.6 us)
Sparse Core Ops, SparseCore 0:
  11.7 66.1 all-gather.14
  81.6 57.6 all-gather.16
  148.1 688.2 all-gather.20
  839.3 60.9 all-gather.18
  903.9 57.6 all-gather.22
  965.2 63.9 all-gather.24
  1062.6 64.4 all-gather.26
